TPU v7x, 128 devices: a whole 4x4x4 slice. The times are simulated.
128 devices in a mesh: freq: 8 (over x_hi, z), cell: 16 (over x_lo, y, core).
Axes of the slice: x: 4 (x_hi: 2, x_lo: 2; x = x_hi * 2 + x_lo), y: 4, z: 4, core: 2. Of those that a mesh axis runs over, the one named last changes fastest.
Arguments:
- green: bfloat16 [2, 16, 1024, 8192], P(None, 'freq', None, 'cell'), may hold values from -0.25 to 0.25
- coeffs: float32 [8, 8192], P('freq', 'cell'), may hold values from -6 to 6
- basis: float32 [16, 8], P('freq'), may hold values from -2 to 2
- amplitude: float32 [16, 1024], P('freq'), may hold values from 0.5 to 2
- block_mask: int32 [16, 16], replicated, may hold values 0 or 1
Outputs:
- hess_vec: float32 [8, 8192], P('freq', 'cell')
All inputs are finite; a program needn't handle non-finite values.
Results may differ from a plain program's by a relative error of at most 0.0024.
Values may be sent and summed in bfloat16 or wider, within the bound.
A program may use at most 192 MiB of HBM per device.

v0:
```python
import jax
import jax.numpy as jnp
from jax import lax
from jax.sharding import PartitionSpec as P

NS = 1024


def from_everyone(value, axis):
    copies = jnp.broadcast_to(value, (lax.axis_size(axis), *value.shape))
    return lax.all_to_all(copies, axis, split_axis=0, concat_axis=0, tiled=True)


def in_order(parts, dim):
    dims = list(parts.shape[1:])
    dims[dim] *= parts.shape[0]
    return jnp.moveaxis(parts, 0, dim).reshape(dims)


def gathered_copies(value, axis, dim):
    parts = from_everyone(value, axis)
    return in_order(parts, dim)


def cut_along(value, dim, count):
    before, after = (value.shape[:dim], value.shape[dim + 1 :])
    return jnp.moveaxis(value.reshape(*before, count, -1, *after), dim, 0)


def summed_on_arrival(value, axis, dim):
    parts = cut_along(value, dim, lax.axis_size(axis))
    arrived = lax.all_to_all(parts, axis, split_axis=0, concat_axis=0, tiled=True)
    return arrived.sum(axis=0)


def whiten(corr, amplitude, expanded):
    weight = amplitude.T[:, :, None] * amplitude[None, :, :] * expanded[:, None, :]
    return (weight[:, :, None, :] * corr).astype(jnp.bfloat16)


def on_device(green, coeffs, basis, amplitude, block_mask):
    highest = lax.Precision.HIGHEST
    full = gathered_copies(coeffs, "freq", 0)
    source = jnp.dot(basis, full, precision=highest)
    scaled = (green * source[None, :, None, :]).astype(jnp.bfloat16)
    right = jnp.stack((jnp.stack((green[0], green[1])), jnp.stack((-green[1], green[0]))))
    blocks = block_mask.shape[0]
    width = NS // blocks
    expanded = (
        jnp.broadcast_to(block_mask[:, None, :, None], (blocks, width, blocks, width))
        .reshape(NS, NS)
        .astype(jnp.float32)
    )
    total = lax.psum(
        jnp.einsum("pfic,qpfjc->ifqj", scaled, right, preferred_element_type=jnp.float32).astype(
            jnp.bfloat16
        ),
        "cell",
    ).astype(jnp.float32)
    resid = whiten(total, amplitude, expanded)
    yre = jnp.einsum("ifj,fjc->fic", resid[:, :, 0], green[0], preferred_element_type=jnp.float32)
    yre = yre - jnp.einsum(
        "ifj,fjc->fic", resid[:, :, 1], green[1], preferred_element_type=jnp.float32
    )
    yim = jnp.einsum("ifj,fjc->fic", resid[:, :, 0], green[1], preferred_element_type=jnp.float32)
    yim = yim + jnp.einsum(
        "ifj,fjc->fic", resid[:, :, 1], green[0], preferred_element_type=jnp.float32
    )
    sens = jnp.sum(green[0] * yre + green[1] * yim, axis=1)
    partial_value = jnp.dot(basis.T, sens, precision=highest)
    return summed_on_arrival(partial_value, "freq", 0)


def solution(mesh):
    placed = (
        P(None, "freq", None, "cell"),
        P("freq", "cell"),
        P("freq", None),
        P("freq", None),
        P(),
    )
    return jax.shard_map(
        on_device, mesh=mesh, in_specs=placed, out_specs=P("freq", "cell"), check_vma=False
    )
```

profile of v0, /device:TPU:1, one launch (start us, length us, event | category | flops | bytes accessed | tf_op | source)
XLA Modules:
  0.0 231.0 jit_solution(13956401974182939878)
XLA Ops:
  6.5 0.0 copy-start
  6.5 1.3 broadcast_in_dim.5
  7.8 8.3 %all-to-all-start = ((f32[8,1,512]{2,1,0:T(1,128)}), f32[8,1,512]{2,1,0:T(1,128)S(1)}, u32[]{:S(2)}, u32[]{:S(2)}) async-start(f32[8,1,512]{2,1,0:T(1,128)} %broadcast_in_dim.5), calls=%async_computation | async-start | bytes 32768 | tf_op jit(solution)/shard_map/all_to_all | solution.py:11
  16.1 0.0 all-reduce.2.cloned.1.call-start
  16.2 0.0 copy-start.1
  16.2 1.9 negate_bitcast_fusion
  18.1 0.9 copy-done.1
  19.0 0.3 copy.30
  19.3 0.0 copy-start.3
  19.3 1.9 copy-done.3
  21.2 0.1 slice.13
  21.4 2.3 maximum_bitcast_fusion
  23.7 0.0 all-to-all-done
  23.7 0.1 fusion.21
  23.8 14.5 %fusion = bf16[1024,2,2,1024]{0,3,2,1:T(8,128)(2,1)} fusion(bf16[1,2,2,1024,512]{4,3,1,0,2:T(8,128)(2,1)} %maximum_bitcast_fusion, bf16[1,2,2,1024,512]{4,3,1,0,2:T(8,128)(2,1)} %bitcast.59, bf16[2,2,1024,512]{3,2,1,0:T(8,128)(2,1)} %param.5, f32[2,512]{1,0:T(2,128)S(1)} %fusion.21), kind=kOutput, calls=%fused_computation.2 | convolution fusion | flops 8604614656 | bytes 20975616 | tf_op jit(solution)/shard_map/pfic,qpfjc->ifqj/dot_general | solution.py:55
  38.4 0.0 all-reduce.2.cloned.1.call-update
  38.4 0.7 copy-done.7
  39.1 0.1 copy.12
  39.1 3.8 %broadcast_in_dim.4 = f32[16,64,16,64]{1,0,3,2:T(8,128)} broadcast(f32[16,16]{0,1:T(8,128)S(1)} %copy.12), dimensions={0,2} | broadcast | bytes 4195328 | tf_op jit(solution)/shard_map/broadcast_in_dim | solution.py:50
  43.0 7.6 %convert_element_type.37 = f32[1024,1024]{0,1:T(8,128)} reshape(f32[16,64,16,64]{1,0,3,2:T(8,128)} %broadcast_in_dim.4) | data formatting | bytes 8388608 | tf_op jit(solution)/shard_map/convert_element_type | solution.py:52
  50.6 5.3 %multiply_multiply_fusion = f32[1024,2,1024]{0,2,1:T(8,128)} fusion(f32[1024,1024]{0,1:T(8,128)} %convert_element_type.37, f32[2,1024]{1,0:T(2,128)S(1)} %copy-done.6, f32[1024,2]{0,1:T(2,128)S(1)} %bitcast.60), kind=kLoop, calls=%fused_computation.8 | loop fusion | flops 4194304 | bytes 12599296 | tf_op jit(solution)/shard_map/mul | solution.py:37
  55.9 125.8 %all-reduce.2.cloned.1.call-done = bf16[1024,2,2,1024]{0,3,2,1:T(8,128)(2,1)} async-done(((bf16[1024,2,2,1024]{0,3,2,1:T(8,128)(2,1)}), bf16[1024,2,2,1024]{0,3,2,1:T(8,128)(2,1)}) %all-reduce.2.cloned.1.call-update) | async-done | bytes 8388624 | tf_op jit(solution)/shard_map/psum | solution.py:54
  181.7 7.6 %multiply_convert_fusion = bf16[1024,2,2,1024]{0,3,2,1:T(8,128)(2,1)S(1)} fusion(bf16[1024,2,2,1024]{0,3,2,1:T(8,128)(2,1)} %all-reduce.2.cloned.1.call-done, f32[1024,2,1024]{0,2,1:T(8,128)} %multiply_multiply_fusion), kind=kLoop, calls=%fused_computation.1 | loop fusion | flops 12582912 | bytes 25165824 | tf_op jit(solution)/shard_map/convert_element_type | solution.py:38
  189.3 0.0 copy-start.2
  189.3 2.4 %fusion.11 = f32[2,1024,512]{2,1,0:T(8,128)S(1)} fusion(bf16[1024,2,2,1024]{0,3,2,1:T(8,128)(2,1)S(1)} %multiply_convert_fusion, bf16[2,2,1024,512]{3,2,0,1:T(8,128)(2,1)S(1)} %copy-done.4), kind=kOutput, calls=%fused_computation.17 | convolution fusion | flops 2147483648 | bytes 10485760 | tf_op jit(solution)/shard_map/ifj,fjc->fic/dot_general | solution.py:66
  191.7 2.8 %copy-done.2 = bf16[2,2,1024,512]{3,2,1,0:T(8,128)(2,1)S(1)} copy-done((bf16[2,2,1024,512]{3,2,1,0:T(8,128)(2,1)S(1)}, bf16[2,2,1024,512]{3,2,1,0:T(8,128)(2,1)}, u32[]{:S(2)}) %copy-start.2) | copy-done | bytes 4194328
  194.5 4.3 %fusion.9 = f32[2,1024,512]{2,1,0:T(8,128)} fusion(bf16[1024,2,2,1024]{0,3,2,1:T(8,128)(2,1)S(1)} %multiply_convert_fusion, bf16[2,2,1024,512]{3,2,1,0:T(8,128)(2,1)S(1)} %copy-done.2), kind=kOutput, calls=%fused_computation.15 | convolution fusion | flops 2147483648 | bytes 10485760 | tf_op jit(solution)/shard_map/ifj,fjc->fic/dot_general | solution.py:65
  198.9 4.3 %fusion.10 = f32[2,1024,512]{2,1,0:T(8,128)} fusion(bf16[1024,2,2,1024]{0,3,2,1:T(8,128)(2,1)S(1)} %multiply_convert_fusion, bf16[2,2,1024,512]{3,2,0,1:T(8,128)(2,1)S(1)} %copy-done.4), kind=kOutput, calls=%fused_computation.16 | convolution fusion | flops 2147483648 | bytes 10485760 | tf_op jit(solution)/shard_map/ifj,fjc->fic/dot_general | solution.py:61
  203.2 7.5 %add_reduce_fusion = f32[2,512]{1,0:T(2,128)S(1)} fusion(f32[2,1024,512]{2,1,0:T(8,128)} %fusion.9, f32[2,1024,512]{2,1,0:T(8,128)S(1)} %fusion.11, f32[2,1024,512]{2,1,0:T(8,128)} %fusion.10, bf16[1024,2,2,1024]{0,3,2,1:T(8,128)(2,1)} %copy-done.5, bf16[2,2,1024,512]{3,2,1,0:T(8,128)(2,1)S(1)} %copy-done.2, bf16[2,2,1024,512]{3,2,0,1:T(8,128)(2,1)S(1)} %copy-done.4), kind=kOutput, calls=%fused_computation.14 | convolution fusion | flops 2155871232 | bytes 23072768 | tf_op jit(solution)/shard_map/ifj,fjc->fic/dot_general | solution.py:62
  210.7 0.2 convolution_bitcast_fusion
  210.9 12.6 %all_to_all.10 = f32[8,1,512]{2,1,0:T(1,128)S(1)} all-to-all(f32[8,1,512]{2,1,0:T(1,128)S(1)} %copy.16), channel_id=1, replica_groups=mesh['freq'=8,'cell'=16] {'freq'}, dimensions={0} | all-to-all | bytes 32768 | tf_op jit(solution)/shard_map/all_to_all | solution.py:32
  223.6 0.6 reduce_sum.21
  (10 shorter events, 0.0 us)
Async XLA Ops:
  6.5 17.1 %copy-start = (f32[2,8]{1,0:T(2,128)S(1)}, f32[2,8]{1,0:T(2,128)}, u32[]{:S(2)}) copy-start(f32[2,8]{1,0:T(2,128)} %param.7) | copy-start | bytes 196
  7.8 15.8 %all-to-all-start = ((f32[8,1,512]{2,1,0:T(1,128)}), f32[8,1,512]{2,1,0:T(1,128)S(1)}, u32[]{:S(2)}, u32[]{:S(2)}) async-start(f32[8,1,512]{2,1,0:T(1,128)} %broadcast_in_dim.5), calls=%async_computation | async-start | bytes 32768 | tf_op jit(solution)/shard_map/all_to_all | solution.py:11
  16.1 165.6 %all-reduce.2.cloned.1.call-start = ((), (), s32[]{:S(2)}) async-start(), calls=%async_computation.2 | async-start | bytes 16777216 | tf_op jit(solution)/shard_map/psum | solution.py:54
  16.2 2.8 %copy-start.1 = (bf16[2,2,1024,512]{3,2,1,0:T(8,128)(2,1)S(1)}, bf16[2,2,1024,512]{3,2,1,0:T(8,128)(2,1)}, u32[]{:S(2)}) copy-start(bf16[2,2,1024,512]{3,2,1,0:T(8,128)(2,1)} %param.5) | copy-start | bytes 12582916
  19.3 1.9 copy-start.3
  38.4 0.7 copy-start.7
  43.0 7.6 %copy-start.6 = (f32[2,1024]{1,0:T(2,128)S(1)}, f32[2,1024]{1,0:T(2,128)}, u32[]{:S(2)}) copy-start(f32[2,1024]{1,0:T(2,128)} %param.8) | copy-start | bytes 24580
  181.7 7.6 %copy-start.4 = (bf16[2,2,1024,512]{3,2,0,1:T(8,128)(2,1)S(1)}, bf16[2,2,1024,512]{3,2,0,1:T(8,128)(2,1)}, u32[]{:S(2)}) copy-start(bf16[2,2,1024,512]{3,2,0,1:T(8,128)(2,1)} %copy-done.3) | copy-start | bytes 12582916
  189.3 9.6 %copy-start.5 = (bf16[1024,2,2,1024]{0,3,2,1:T(8,128)(2,1)}, bf16[1024,2,2,1024]{0,3,2,1:T(8,128)(2,1)S(1)}, u32[]{:S(2)}) copy-start(bf16[1024,2,2,1024]{0,3,2,1:T(8,128)(2,1)S(1)} %multiply_convert_fusion) | copy-start | bytes 25165828
  189.3 5.2 %copy-start.2 = (bf16[2,2,1024,512]{3,2,1,0:T(8,128)(2,1)S(1)}, bf16[2,2,1024,512]{3,2,1,0:T(8,128)(2,1)}, u32[]{:S(2)}) copy-start(bf16[2,2,1024,512]{3,2,1,0:T(8,128)(2,1)} %param.5) | copy-start | bytes 12582916
Sparse Core Ops, SparseCore 0:
  38.5 143.1 all-reduce.1
where the time goes:
time: 234 us; the launch traced here: 231 us
  waiting for transfers between devices  126 us (54%)
  matrix products  33.4 us (14%)
  local copies, waits for them, and re-layouts  19.6 us (8%)
  other arithmetic  17.7 us (8%)
  between operations  13.5 us (6%)
  blocking collectives  12.6 us (5%)
  starting transfers between devices  8.35 us (4%)
    psum x1, waiting for transfers between devices, on_device(): lax.psum(jnp.einsum('pfic,qpfjc->ifqj', scaled, right, preferred_element_...  126 us
    dot_general x1, matrix products, on_device(): jnp.einsum('pfic,qpfjc->ifqj', scaled, right, preferred_element_type=jnp....  14.5 us
    all_to_all x1, blocking collectives, summed_on_arrival(): lax.all_to_all(parts, axis, split_axis=0, concat_axis=0, tiled=True)  12.6 us
    all_to_all x1, starting transfers between devices, from_everyone(): return lax.all_to_all(copies, axis, split_axis=0, concat_axis=0, tiled=True)  8.31 us
    convert_element_type x2, local copies, waits for them, and re-layouts, on_device(): expanded = jnp.broadcast_to(block_mask[:, None, :, None], (blocks, width,...  7.69 us
    convert_element_type x1, other arithmetic, whiten(): return (weight[:, :, None, :] * corr).astype(jnp.bfloat16)  7.57 us
    dot_general x1, matrix products, on_device(): jnp.einsum('ifj,fjc->fic', resid[:, :, 1], green[1], preferred_element_ty...  7.54 us
    unnamed x17, local copies, waits for them, and re-layouts  6.66 us
  transfers between devices with their start and end apart: 2, of which 1 were waited for; matrix products, arithmetic and copies ran while one was open for 9% of the time, Pallas kernels for 0%

commit v1 on v0

v1 whole, which is shorter than its diff:
```python
import functools

import jax
import jax.numpy as jnp
from jax import lax
from jax.experimental import pallas as pl
from jax.experimental.pallas import tpu as pltpu
from jax.sharding import PartitionSpec as P

MESH = pl.DeviceIdType.MESH
F32, BF16 = jnp.float32, jnp.bfloat16
NS = 1024
WAVES = 4
ROWS = NS // WAVES
UNIT = ROWS // 8
BLOCKS = 16
WIDTH = NS // BLOCKS


def dot_nt(a, b):
    return lax.dot_general(a, b, (((1,), (1,)), ((), ())), preferred_element_type=F32)


def dot_nn(a, b):
    return lax.dot_general(a, b, (((1,), (0,)), ((), ())), preferred_element_type=F32)


def kernel(
    nfreq,
    green,
    coeffs,
    basis,
    amp,
    mask,
    out,
    g,
    cbuf,
    sc,
    part,
    m1,
    m2,
    m3,
    relay,
    xsend,
    xrecv,
    keep,
    resid,
    weight,
    sens,
    fsend,
    frecv,
    own_sem,
    swap_send,
    swap_recv,
    c_send,
    c_recv,
    rs_send,
    rs_recv,
    ag_send,
    ag_recv,
    f_send,
    f_recv,
):
    q = lax.axis_index("freq")
    cell = lax.axis_index("cell")
    core = lax.rem(cell, 2)
    y = lax.rem(lax.div(cell, 2), 4)
    x = lax.div(cell, 8)
    yp, ym, y2 = lax.rem(y + 1, 4), lax.rem(y + 3, 4), lax.rem(y + 2, 4)

    def at(x_, y_, core_):
        return {"freq": q, "cell": x_ * 8 + y_ * 2 + core_}

    up, down = at(x, yp, core), at(x, ym, core)
    across, twin = at(1 - x, y, core), at(x, y, 1 - core)

    peers = [(d, h) for d in range(nfreq) for h in range(2) if (d, h) != (0, 0)]

    def peer(d, h):
        to_core = core if h == 0 else 1 - core
        to_q = lax.rem(q + d, nfreq)
        return {"freq": to_q, "cell": x * 8 + y * 2 + to_core}

    def remote(src, dst, send, recv, device):
        return pltpu.make_async_remote_copy(
            src_ref=src,
            dst_ref=dst,
            send_sem=send,
            recv_sem=recv,
            device_id=device,
            device_id_type=MESH,
        )

    own = [pltpu.make_async_copy(green.at[p, core], g.at[0, p], own_sem.at[p]) for p in range(2)]
    for copy in own:
        copy.start()

    barrier = pltpu.get_barrier_semaphore()
    met = [peer(d, h) for d, h in peers] + [up, down, across]
    for device in met:
        pl.semaphore_signal(barrier, inc=1, device_id=device, device_id_type=MESH)

    lane = lax.broadcasted_iota(jnp.int32, (1, NS), 1)
    block_of = lane // WIDTH
    amp_row = amp[pl.ds(core, 1), :]
    for w in range(WAVES):
        first = w * ROWS + (y * 2 + x) * UNIT
        a = lax.div(first, WIDTH)
        pair = jnp.zeros((1, NS), F32)
        for b in range(BLOCKS):
            m = (mask[a, b] + mask[b, a]).astype(F32)
            pair = pair + jnp.where(block_of == b, m, 0.0)
        row = lax.broadcasted_iota(jnp.int32, (UNIT, NS), 0) + first
        col = lax.broadcasted_iota(jnp.int32, (UNIT, NS), 1)
        same = row == col
        amp_col = jnp.sum(jnp.where(same, amp_row, 0.0), axis=1, keepdims=True)
        weight[w] = jnp.where(same, 0.5, 1.0) * (amp_col * (amp_row * pair))

    pl.semaphore_wait(barrier, len(met))

    c_copies = []
    for n, (d, h) in enumerate(peers):
        c_copies.append(
            remote(coeffs, cbuf.at[q, h], c_send.at[n], c_recv.at[n], peer(d, h))
        )
        c_copies[-1].start()
    swap = [
        remote(green.at[p, 1 - core], g.at[1, p], swap_send.at[p], swap_recv.at[p], twin)
        for p in range(2)
    ]
    for copy in swap:
        copy.start()
    cbuf[q, 0] = coeffs[...]

    for copy in c_copies:
        copy.wait_recv()
    source = []
    for h in range(2):
        total = basis[core, 0] * cbuf[0, h]
        for b in range(1, nfreq):
            total = total + basis[core, b] * cbuf[b, h]
        source.append(total)

    for copy in own:
        copy.wait()
    for copy in swap:
        copy.wait_recv()

    sent = []

    def start(copy):
        copy.start()
        sent.append(copy)

    def rs_up(w, n, src, dst):
        return remote(src, dst, rs_send.at[w, n, 0], rs_recv.at[w, n, 0], up)

    def rs_down(w, n, src, dst):
        return remote(src, dst, rs_send.at[w, n, 1], rs_recv.at[w, n, 1], down)

    def ag(w, n, unit, device):
        ref = resid.at[w, unit]
        return remote(ref, ref, ag_send.at[w, n], ag_recv.at[w, unit], device)

    def produce(w):
        rows = pl.ds(w * ROWS, ROWS)
        for h in range(2):
            for p in range(2):
                sc[h, p] = (g[h, p, rows, :].astype(F32) * source[h]).astype(BF16)

        def real(j):
            cols = pl.ds(j * ROWS, ROWS)
            total = dot_nt(sc[0, 0], g[0, 0, cols, :])
            total += dot_nt(sc[0, 1], g[0, 1, cols, :])
            total += dot_nt(sc[1, 0], g[1, 0, cols, :])
            total += dot_nt(sc[1, 1], g[1, 1, cols, :])
            return total

        def imag(j):
            cols = pl.ds(j * ROWS, ROWS)
            plus = dot_nt(sc[0, 1], g[0, 0, cols, :])
            plus += dot_nt(sc[1, 1], g[1, 0, cols, :])
            minus = dot_nt(sc[0, 0], g[0, 1, cols, :])
            minus += dot_nt(sc[1, 0], g[1, 1, cols, :])
            return plus - minus

        def put(j, block):
            part[w, :, :, pl.ds(j * ROWS, ROWS)] = block.astype(BF16).reshape(8, UNIT, ROWS)

        for j in range(w):
            put(j, imag(j))
        i_ = lax.broadcasted_iota(jnp.int32, (ROWS, ROWS), 0)
        j_ = lax.broadcasted_iota(jnp.int32, (ROWS, ROWS), 1)
        put(w, jnp.where(i_ <= j_, real(w), imag(w)))
        for j in range(w + 1, WAVES):
            put(j, real(j))
        start(rs_up(w, 0, part.at[w, y2 * 2], m1.at[w, 0]))
        start(rs_down(w, 0, part.at[w, y2 * 2 + 1], m1.at[w, 1]))
        start(rs_up(w, 1, part.at[w, yp * 2 + 1], m2.at[w, 0]))
        start(rs_down(w, 1, part.at[w, ym * 2], m2.at[w, 1]))

    def pass_on(w):
        rs_up(w, 0, part.at[w, y2 * 2], m1.at[w, 0]).wait_recv()
        relay[w, 0] = (part[w, yp * 2].astype(F32) + m1[w, 0].astype(F32)).astype(BF16)
        start(rs_up(w, 2, relay.at[w, 0], m3.at[w, 0]))
        rs_down(w, 0, part.at[w, y2 * 2 + 1], m1.at[w, 1]).wait_recv()
        relay[w, 1] = (part[w, ym * 2 + 1].astype(F32) + m1[w, 1].astype(F32)).astype(BF16)
        start(rs_down(w, 2, relay.at[w, 1], m3.at[w, 1]))

    def cross(w):
        return remote(xsend.at[w], xrecv.at[w], rs_send.at[w, 3, 0], rs_recv.at[w, 3, 0], across)

    def collect(w):
        rs_up(w, 1, part.at[w, yp * 2 + 1], m2.at[w, 0]).wait_recv()
        rs_down(w, 1, part.at[w, ym * 2], m2.at[w, 1]).wait_recv()
        rs_up(w, 2, relay.at[w, 0], m3.at[w, 0]).wait_recv()
        rs_down(w, 2, relay.at[w, 1], m3.at[w, 1]).wait_recv()
        low = part[w, y * 2].astype(F32) + m3[w, 0].astype(F32) + m2[w, 1].astype(F32)
        high = part[w, y * 2 + 1].astype(F32) + m3[w, 1].astype(F32) + m2[w, 0].astype(F32)
        mine = x == 0
        xsend[w] = jnp.where(mine, high, low).astype(BF16)
        start(cross(w))
        keep[w] = jnp.where(mine, low, high)

    def finish(w):
        cross(w).wait_recv()
        unit = y * 2 + x
        resid[w, unit] = (weight[w] * (keep[w] + xrecv[w].astype(F32))).astype(BF16)
        start(ag(w, 0, unit, across))
        start(ag(w, 1, unit, up))
        start(ag(w, 2, unit, down))

    def share(w):
        unit = y * 2 + 1 - x
        ag(w, 0, unit, across).wait_recv()
        start(ag(w, 3, unit, up))
        start(ag(w, 4, unit, down))

    def forward(w):
        ag(w, 1, ym * 2, up).wait_recv()
        start(ag(w, 5, ym * 2, up))
        ag(w, 1, yp * 2 + 1, down).wait_recv()
        start(ag(w, 6, yp * 2 + 1, down))

    def consume(w):
        for unit in (ym * 2 + 1, yp * 2, y2 * 2, y2 * 2 + 1):
            ag(w, 1, unit, up).wait_recv()
        block = resid[w].reshape(ROWS, NS)
        i_ = lax.broadcasted_iota(jnp.int32, (ROWS, ROWS), 0)
        j_ = lax.broadcasted_iota(jnp.int32, (ROWS, ROWS), 1)
        lo, hi = w * ROWS, (w + 1) * ROWS
        middle = block[:, lo:hi]
        zero = jnp.zeros_like(middle)
        upper = jnp.where(i_ <= j_, middle, zero)
        lower = jnp.where(i_ > j_, middle, zero)
        if w + 1 < WAVES:
            upper = jnp.concatenate([upper, block[:, hi:]], axis=1)
        if w > 0:
            lower = jnp.concatenate([block[:, :lo], lower], axis=1)
        rows = pl.ds(lo, ROWS)
        width = g.shape[3]
        step = min(256, width)
        for h in range(2):
            for t in range(width // step):
                cols = pl.ds(t * step, step)
                gr_u, gi_u = g[h, 0, lo:, cols], g[h, 1, lo:, cols]
                gr_l, gi_l = g[h, 0, :hi, cols], g[h, 1, :hi, cols]
                zr = dot_nn(upper, gr_u) - dot_nn(lower, gi_l)
                zi = dot_nn(upper, gi_u) + dot_nn(lower, gr_l)
                value = g[h, 0, rows, cols].astype(F32) * zr + g[h, 1, rows, cols].astype(F32) * zi
                value = jnp.sum(value, axis=0, keepdims=True)
                if w > 0:
                    value = value + sens[h, :, cols]
                sens[h, :, cols] = value

    stages = (produce, pass_on, collect, finish, share, forward, consume)
    for slot in range(WAVES + len(stages) - 1):
        for s, stage in enumerate(stages):
            if 0 <= slot - s < WAVES:
                stage(slot - s)

    f_copies = []
    me = q * 2 + core
    for n, (d, h) in enumerate(peers):
        to_q = lax.rem(q + d, nfreq)
        fsend[n] = basis[core, to_q] * sens[h]
        f_copies.append(remote(fsend.at[n], frecv.at[me], f_send.at[n], f_recv.at[n], peer(d, h)))
        f_copies[-1].start()
    frecv[me] = basis[core, q] * sens[0]
    for copy in f_copies:
        copy.wait_recv()
    total = frecv[0]
    for n in range(1, 2 * nfreq):
        total = total + frecv[n]
    out[...] = total

    for copy in c_copies + swap + sent + f_copies:
        copy.wait_send()


def on_device(green, coeffs, basis, amplitude, block_mask):
    nfreq = lax.axis_size("freq")
    cells = green.shape[3]
    dma = pltpu.SemaphoreType.DMA
    n = 2 * nfreq - 1
    return pl.pallas_call(
        functools.partial(kernel, nfreq),
        out_shape=jax.ShapeDtypeStruct((1, cells), F32),
        in_specs=[
            pl.BlockSpec(memory_space=pl.ANY),
            pl.BlockSpec(memory_space=pltpu.VMEM),
            pl.BlockSpec(memory_space=pltpu.SMEM),
            pl.BlockSpec(memory_space=pltpu.VMEM),
            pl.BlockSpec(memory_space=pltpu.SMEM),
        ],
        out_specs=pl.BlockSpec(memory_space=pltpu.VMEM),
        scratch_shapes=[
            pltpu.VMEM((2, 2, NS, cells), BF16),
            pltpu.VMEM((nfreq, 2, 1, cells), F32),
            pltpu.VMEM((2, 2, ROWS, cells), BF16),
            pltpu.VMEM((WAVES, 8, UNIT, NS), BF16),
            pltpu.VMEM((WAVES, 2, UNIT, NS), BF16),
            pltpu.VMEM((WAVES, 2, UNIT, NS), BF16),
            pltpu.VMEM((WAVES, 2, UNIT, NS), BF16),
            pltpu.VMEM((WAVES, 2, UNIT, NS), BF16),
            pltpu.VMEM((WAVES, UNIT, NS), BF16),
            pltpu.VMEM((WAVES, UNIT, NS), BF16),
            pltpu.VMEM((WAVES, UNIT, NS), F32),
            pltpu.VMEM((WAVES, 8, UNIT, NS), BF16),
            pltpu.VMEM((WAVES, UNIT, NS), F32),
            pltpu.VMEM((2, 1, cells), F32),
            pltpu.VMEM((n, 1, cells), F32),
            pltpu.VMEM((2 * nfreq, 1, cells), F32),
            dma((2,)),
            dma((2,)),
            dma((2,)),
            dma((n,)),
            dma((n,)),
            dma((WAVES, 4, 2)),
            dma((WAVES, 4, 2)),
            dma((WAVES, 7)),
            dma((WAVES, 8)),
            dma((n,)),
            dma((n,)),
        ],
        compiler_params=pltpu.CompilerParams(
            collective_id=0, has_side_effects=True, vmem_limit_bytes=48 * 1024 * 1024
        ),
        name="hessian_vector",
    )(green, coeffs, basis, amplitude, block_mask)


def solution(mesh):
    placed = (
        P(None, "freq", None, "cell"),
        P("freq", "cell"),
        P("freq", None),
        P("freq", None),
        P(),
    )
    return jax.shard_map(
        on_device, mesh=mesh, in_specs=placed, out_specs=P("freq", "cell"), check_vma=False
    )
```

time: 234 us -> 68.8 us (0.29); the launches traced: 231 us -> 68.6 us
  waiting for transfers between devices: 126 us -> 0 us
  Pallas kernels: 0 us -> 63 us
  matrix products: 33.4 us -> 0 us
  other arithmetic: 17.7 us -> 0 us
  local copies, waits for them, and re-layouts: 19.6 us -> 5.52 us
  between operations: 13.5 us -> 0.01 us
  blocking collectives: 12.6 us -> 0 us
  starting transfers between devices: 8.35 us -> 0 us
    psum x1 -> x0, waiting for transfers between devices: 126 us -> none  [on_device(): lax.psum(jnp.einsum('pfic,qpfjc->ifqj', scaled, right, preferred_element_...]
    pallas_call x0 -> x1, Pallas kernels: none -> 63 us  [on_device(): pl.pallas_call(functools.partial(kernel, nfreq), out_shape=jax.ShapeDtype...]
    dot_general x7 -> x0, matrix products: 33.4 us -> none  [the longest x1 14.5 us: on_device(): jnp.einsum('pfic,qpfjc->ifqj', scaled, right, preferred_element_type=jnp....]
    all_to_all x1 -> x0, blocking collectives: 12.6 us -> none  [summed_on_arrival(): lax.all_to_all(parts, axis, split_axis=0, concat_axis=0, tiled=True)]
    all_to_all x1 -> x0, starting transfers between devices: 8.31 us -> none  [from_everyone(): return lax.all_to_all(copies, axis, split_axis=0, concat_axis=0, tiled=True)]
    convert_element_type x2 -> x0, local copies, waits for them, and re-layouts: 7.69 us -> none  [on_device(): expanded = jnp.broadcast_to(block_mask[:, None, :, None], (blocks, width,...]
    convert_element_type x2 -> x0, other arithmetic: 7.57 us -> none  [the longest x1 7.57 us: whiten(): return (weight[:, :, None, :] * corr).astype(jnp.bfloat16)]
    mul x1 -> x0, other arithmetic: 5.35 us -> none  [whiten(): amplitude.T[:, :, None] * amplitude[None, :, :] * expanded[:, None, :]]
  transfers between devices with their start and end apart: 2 -> 0, of which waited for: 1 -> 0; matrix products, arithmetic and copies ran while one was open for 9% -> 0% of each run, Pallas kernels for 0% -> 0%
where the time goes in v1:
time: 68.8 us; the launch traced here: 68.6 us
  Pallas kernels  63 us (92%)
  local copies, waits for them, and re-layouts  5.52 us (8%)
    pallas_call x1, Pallas kernels, on_device(): pl.pallas_call(functools.partial(kernel, nfreq), out_shape=jax.ShapeDtype...  63 us
    unnamed x11, local copies, waits for them, and re-layouts  5.52 us

profile of v1, /device:TPU:1, one launch (start us, length us, event | category | flops | bytes accessed | tf_op | source)
XLA Modules:
  0.0 68.6 jit_solution(7298214575515112771)
XLA Ops:
  0.0 0.0 copy-start
  0.0 2.2 %copy-done = bf16[2,2,1024,512]{3,2,1,0:T(8,128)(2,1)S(1)} copy-done((bf16[2,2,1024,512]{3,2,1,0:T(8,128)(2,1)S(1)}, bf16[2,2,1024,512]{3,2,1,0:T(8,128)(2,1)}, u32[]{:S(2)}) %copy-start) | copy-done | bytes 4194328
  2.2 0.0 copy-start.1
  2.2 0.7 %copy-done.1 = f32[2,1024]{1,0:T(2,128)S(1)} copy-done((f32[2,1024]{1,0:T(2,128)S(1)}, f32[2,1024]{1,0:T(2,128)}, u32[]{:S(2)}) %copy-start.1) | copy-done | bytes 8216
  2.9 0.0 copy-start.2
  2.9 0.7 %copy-done.2 = s32[16,16]{1,0:T(8,128)S(1)} copy-done((s32[16,16]{1,0:T(8,128)S(1)}, s32[16,16]{1,0:T(8,128)}, u32[]{:S(2)}) %copy-start.2) | copy-done | bytes 1048
  3.6 0.0 copy-start.3
  3.6 0.7 copy-done.3
  4.3 0.0 copy-start.4
  4.3 0.7 copy-done.4
  4.9 63.0 %hessian_vector.1 = f32[1,512]{1,0:T(1,128)S(1)} custom-call(bf16[2,2,1024,512]{3,2,1,0:T(8,128)(2,1)S(1)} %copy-done, f32[1,512]{1,0:T(1,128)S(1)} %copy-done.3, f32[2,8]{1,0:T(2,128)S(1)} %copy-done.4, f32[2,1024]{1,0:T(2,128)S(1)} %copy-done.1, s32[16,16]{1,0:T(8,128)S(1)} %copy-done.2), custom_call_target="tpu_custom_call" | custom-call | tf_op jit(solution)/shard_map/hessian_vector/pallas_call | solution.py:306
  68.0 0.6 copy.7
Async XLA Ops:
  0.0 2.2 %copy-start = (bf16[2,2,1024,512]{3,2,1,0:T(8,128)(2,1)S(1)}, bf16[2,2,1024,512]{3,2,1,0:T(8,128)(2,1)}, u32[]{:S(2)}) copy-start(bf16[2,2,1024,512]{3,2,1,0:T(8,128)(2,1)} %green.1) | copy-start | bytes 12582916
  2.2 0.7 %copy-start.1 = (f32[2,1024]{1,0:T(2,128)S(1)}, f32[2,1024]{1,0:T(2,128)}, u32[]{:S(2)}) copy-start(f32[2,1024]{1,0:T(2,128)} %amp.1) | copy-start | bytes 24580
  2.9 0.7 %copy-start.2 = (s32[16,16]{1,0:T(8,128)S(1)}, s32[16,16]{1,0:T(8,128)}, u32[]{:S(2)}) copy-start(s32[16,16]{1,0:T(8,128)} %mask.1) | copy-start | bytes 3076
  3.6 0.7 copy-start.3
  4.3 0.7 copy-start.4

commit v2 on v1

--- a/solution.py
+++ b/solution.py
@@ -10,9 +10,12 @@
 MESH = pl.DeviceIdType.MESH
 F32, BF16 = jnp.float32, jnp.bfloat16
 NS = 1024
-WAVES = 4
-ROWS = NS // WAVES
+ROWS = 128
 UNIT = ROWS // 8
+HALF = NS // 2
+KINDS = "ABABABAB"
+GROUPS = ((0, 2), (2, 4), (4, 6), (6, 8))
+CHUNKS = len(KINDS)
 BLOCKS = 16
 WIDTH = NS // BLOCKS
 
@@ -29,26 +32,37 @@
     nfreq,
     green,
     coeffs,
+    basis_in,
+    amp_in,
+    mask_in,
+    out,
     basis,
     amp,
     mask,
-    out,
     g,
     cbuf,
     sc,
     part,
+    resid,
+    weight,
+    keep,
     m1,
     m2,
     m3,
     relay,
     xsend,
     xrecv,
-    keep,
-    resid,
-    weight,
+    bx,
+    bsum,
+    b1,
+    b2,
+    b3,
+    bhold,
+    brelay,
     sens,
     fsend,
     frecv,
+    in_sem,
     own_sem,
     swap_send,
     swap_recv,
@@ -58,6 +72,12 @@
     rs_recv,
     ag_send,
     ag_recv,
+    bx_send,
+    bx_recv,
+    by_send,
+    by_recv,
+    bg_send,
+    bg_recv,
     f_send,
     f_recv,
 ):
@@ -91,6 +111,14 @@
             device_id_type=MESH,
         )
 
+    small = [
+        pltpu.make_async_copy(basis_in, basis, in_sem.at[0]),
+        pltpu.make_async_copy(amp_in, amp, in_sem.at[1]),
+        pltpu.make_async_copy(mask_in, mask, in_sem.at[2]),
+        pltpu.make_async_copy(coeffs, cbuf.at[q, 0], in_sem.at[3]),
+    ]
+    for copy in small:
+        copy.start()
     own = [pltpu.make_async_copy(green.at[p, core], g.at[0, p], own_sem.at[p]) for p in range(2)]
     for copy in own:
         copy.start()
@@ -100,10 +128,13 @@
     for device in met:
         pl.semaphore_signal(barrier, inc=1, device_id=device, device_id_type=MESH)
 
+    for copy in small:
+        copy.wait()
+
     lane = lax.broadcasted_iota(jnp.int32, (1, NS), 1)
     block_of = lane // WIDTH
     amp_row = amp[pl.ds(core, 1), :]
-    for w in range(WAVES):
+    for w in range(CHUNKS):
         first = w * ROWS + (y * 2 + x) * UNIT
         a = lax.div(first, WIDTH)
         pair = jnp.zeros((1, NS), F32)
@@ -130,7 +161,6 @@
     ]
     for copy in swap:
         copy.start()
-    cbuf[q, 0] = coeffs[...]
 
     for copy in c_copies:
         copy.wait_recv()
@@ -162,42 +192,134 @@
         ref = resid.at[w, unit]
         return remote(ref, ref, ag_send.at[w, n], ag_recv.at[w, unit], device)
 
-    def produce(w):
-        rows = pl.ds(w * ROWS, ROWS)
+    def produce(group):
+        c0, c1 = group
+        lo, hi = c0 * ROWS, c1 * ROWS
+        count = hi - lo
         for h in range(2):
             for p in range(2):
-                sc[h, p] = (g[h, p, rows, :].astype(F32) * source[h]).astype(BF16)
-
-        def real(j):
-            cols = pl.ds(j * ROWS, ROWS)
-            total = dot_nt(sc[0, 0], g[0, 0, cols, :])
-            total += dot_nt(sc[0, 1], g[0, 1, cols, :])
-            total += dot_nt(sc[1, 0], g[1, 0, cols, :])
-            total += dot_nt(sc[1, 1], g[1, 1, cols, :])
+                field = g[h, p, lo:hi, :].astype(F32)
+                sc[h, p, :count, :] = (field * source[h]).astype(BF16)
+
+        def real(start, stop):
+            total = dot_nt(sc[0, 0, :count], g[0, 0, start:stop])
+            total += dot_nt(sc[0, 1, :count], g[0, 1, start:stop])
+            total += dot_nt(sc[1, 0, :count], g[1, 0, start:stop])
+            total += dot_nt(sc[1, 1, :count], g[1, 1, start:stop])
             return total
 
-        def imag(j):
-            cols = pl.ds(j * ROWS, ROWS)
-            plus = dot_nt(sc[0, 1], g[0, 0, cols, :])
-            plus += dot_nt(sc[1, 1], g[1, 0, cols, :])
-            minus = dot_nt(sc[0, 0], g[0, 1, cols, :])
-            minus += dot_nt(sc[1, 0], g[1, 1, cols, :])
+        def imag(start, stop):
+            plus = dot_nt(sc[0, 1, :count], g[0, 0, start:stop])
+            plus += dot_nt(sc[1, 1, :count], g[1, 0, start:stop])
+            minus = dot_nt(sc[0, 0, :count], g[0, 1, start:stop])
+            minus += dot_nt(sc[1, 0, :count], g[1, 1, start:stop])
             return plus - minus
 
-        def put(j, block):
-            part[w, :, :, pl.ds(j * ROWS, ROWS)] = block.astype(BF16).reshape(8, UNIT, ROWS)
-
-        for j in range(w):
-            put(j, imag(j))
-        i_ = lax.broadcasted_iota(jnp.int32, (ROWS, ROWS), 0)
-        j_ = lax.broadcasted_iota(jnp.int32, (ROWS, ROWS), 1)
-        put(w, jnp.where(i_ <= j_, real(w), imag(w)))
-        for j in range(w + 1, WAVES):
-            put(j, real(j))
+        def put(start, stop, block):
+            shape = (c1 - c0, 8, UNIT, stop - start)
+            part[c0:c1, :, :, start:stop] = block.astype(BF16).reshape(shape)
+
+        for start in range(0, lo, 256):
+            stop = min(start + 256, lo)
+            put(start, stop, imag(start, stop))
+        i_ = lax.broadcasted_iota(jnp.int32, (count, count), 0)
+        j_ = lax.broadcasted_iota(jnp.int32, (count, count), 1)
+        put(lo, hi, jnp.where(i_ <= j_, real(lo, hi), imag(lo, hi)))
+        for start in range(hi, NS, 256):
+            stop = min(start + 256, NS)
+            put(start, stop, real(start, stop))
+        for c in range(c0, c1):
+            if KINDS[c] == "A":
+                start_a(c)
+            else:
+                start_b(c)
+
+    def start_a(w):
         start(rs_up(w, 0, part.at[w, y2 * 2], m1.at[w, 0]))
         start(rs_down(w, 0, part.at[w, y2 * 2 + 1], m1.at[w, 1]))
         start(rs_up(w, 1, part.at[w, yp * 2 + 1], m2.at[w, 0]))
         start(rs_down(w, 1, part.at[w, ym * 2], m2.at[w, 1]))
+
+    targets = (y2, yp, ym, y)
+
+    def b_cross(w, r):
+        src = part.at[w, targets[r] * 2 + 1 - x]
+        return remote(src, bx.at[w, r], bx_send.at[w, r], bx_recv.at[w, r], across)
+
+    def b_up(w, n, src, dst):
+        return remote(src, dst, by_send.at[w, n, 0], by_recv.at[w, n, 0], up)
+
+    def b_down(w, n, src, dst):
+        return remote(src, dst, by_send.at[w, n, 1], by_recv.at[w, n, 1], down)
+
+    def left(ref):
+        return ref.at[:, 0:HALF]
+
+    def right(ref):
+        return ref.at[:, HALF:NS]
+
+    def b_share(w, role, ref, device):
+        return remote(ref, ref, bg_send.at[w, role], bg_recv.at[w, role], device)
+
+    def b_unit(w, t):
+        return resid.at[w, t * 2 + x]
+
+    def start_b(w):
+        for r in range(4):
+            start(b_cross(w, r))
+
+    def b_sum(w):
+        def total(r):
+            b_cross(w, r).wait_recv()
+            return part[w, targets[r] * 2 + x].astype(F32) + bx[w, r].astype(F32)
+
+        bsum[w, 0] = total(0).astype(BF16)
+        start(b_up(w, 0, left(bsum.at[w, 0]), b1.at[w, 0]))
+        start(b_down(w, 0, right(bsum.at[w, 0]), b1.at[w, 1]))
+        value = total(1)
+        bhold[w, 0] = value[:, :HALF]
+        bsum[w, 1, :, HALF:] = value[:, HALF:].astype(BF16)
+        start(b_up(w, 1, right(bsum.at[w, 1]), b2.at[w, 0]))
+        value = total(2)
+        bhold[w, 1] = value[:, HALF:]
+        bsum[w, 2, :, :HALF] = value[:, :HALF].astype(BF16)
+        start(b_down(w, 1, left(bsum.at[w, 2]), b2.at[w, 1]))
+        keep[w] = total(3)
+
+    def b_pass_on(w):
+        b_up(w, 0, left(bsum.at[w, 0]), b1.at[w, 0]).wait_recv()
+        brelay[w, 0] = (bhold[w, 0] + b1[w, 0].astype(F32)).astype(BF16)
+        start(b_up(w, 2, brelay.at[w, 0], b3.at[w, 0]))
+        b_down(w, 0, right(bsum.at[w, 0]), b1.at[w, 1]).wait_recv()
+        brelay[w, 1] = (bhold[w, 1] + b1[w, 1].astype(F32)).astype(BF16)
+        start(b_down(w, 2, brelay.at[w, 1], b3.at[w, 1]))
+
+    def b_finish(w):
+        b_up(w, 1, right(bsum.at[w, 1]), b2.at[w, 0]).wait_recv()
+        b_down(w, 1, left(bsum.at[w, 2]), b2.at[w, 1]).wait_recv()
+        b_up(w, 2, brelay.at[w, 0], b3.at[w, 0]).wait_recv()
+        b_down(w, 2, brelay.at[w, 1], b3.at[w, 1]).wait_recv()
+        low = keep[w, :, :HALF] + b3[w, 0].astype(F32) + b2[w, 1].astype(F32)
+        high = keep[w, :, HALF:] + b3[w, 1].astype(F32) + b2[w, 0].astype(F32)
+        unit = y * 2 + x
+        resid[w, unit, :, :HALF] = (weight[w, :, :HALF] * low).astype(BF16)
+        resid[w, unit, :, HALF:] = (weight[w, :, HALF:] * high).astype(BF16)
+        start(b_share(w, 0, b_unit(w, y), up))
+        start(b_share(w, 1, b_unit(w, y), down))
+        start(b_share(w, 4, b_unit(w, y), across))
+
+    def b_forward(w):
+        b_share(w, 0, b_unit(w, ym), up).wait_recv()
+        start(b_share(w, 2, left(b_unit(w, ym)), up))
+        start(b_share(w, 5, b_unit(w, ym), across))
+        b_share(w, 1, b_unit(w, yp), down).wait_recv()
+        start(b_share(w, 3, right(b_unit(w, yp)), down))
+        start(b_share(w, 6, b_unit(w, yp), across))
+
+    def b_last(w):
+        b_share(w, 2, left(b_unit(w, y2)), up).wait_recv()
+        b_share(w, 3, right(b_unit(w, y2)), down).wait_recv()
+        start(b_share(w, 7, b_unit(w, y2), across))
 
     def pass_on(w):
         rs_up(w, 0, part.at[w, y2 * 2], m1.at[w, 0]).wait_recv()
@@ -242,42 +364,65 @@
         ag(w, 1, yp * 2 + 1, down).wait_recv()
         start(ag(w, 6, yp * 2 + 1, down))
 
-    def consume(w):
-        for unit in (ym * 2 + 1, yp * 2, y2 * 2, y2 * 2 + 1):
-            ag(w, 1, unit, up).wait_recv()
-        block = resid[w].reshape(ROWS, NS)
-        i_ = lax.broadcasted_iota(jnp.int32, (ROWS, ROWS), 0)
-        j_ = lax.broadcasted_iota(jnp.int32, (ROWS, ROWS), 1)
-        lo, hi = w * ROWS, (w + 1) * ROWS
+    def arrived(w):
+        if KINDS[w] == "A":
+            for unit in (ym * 2 + 1, yp * 2, y2 * 2, y2 * 2 + 1):
+                ag(w, 1, unit, up).wait_recv()
+        else:
+            for role in range(4, 8):
+                b_share(w, role, b_unit(w, y), across).wait_recv()
+
+    def consume(group):
+        c0, c1 = group
+        lo, hi = c0 * ROWS, c1 * ROWS
+        count = hi - lo
+        for c in range(c0, c1):
+            arrived(c)
+        block = resid[c0:c1].reshape(count, NS)
+        i_ = lax.broadcasted_iota(jnp.int32, (count, count), 0)
+        j_ = lax.broadcasted_iota(jnp.int32, (count, count), 1)
         middle = block[:, lo:hi]
         zero = jnp.zeros_like(middle)
         upper = jnp.where(i_ <= j_, middle, zero)
         lower = jnp.where(i_ > j_, middle, zero)
-        if w + 1 < WAVES:
+        if hi < NS:
             upper = jnp.concatenate([upper, block[:, hi:]], axis=1)
-        if w > 0:
+        if lo > 0:
             lower = jnp.concatenate([block[:, :lo], lower], axis=1)
-        rows = pl.ds(lo, ROWS)
         width = g.shape[3]
         step = min(256, width)
         for h in range(2):
             for t in range(width // step):
-                cols = pl.ds(t * step, step)
-                gr_u, gi_u = g[h, 0, lo:, cols], g[h, 1, lo:, cols]
-                gr_l, gi_l = g[h, 0, :hi, cols], g[h, 1, :hi, cols]
-                zr = dot_nn(upper, gr_u) - dot_nn(lower, gi_l)
-                zi = dot_nn(upper, gi_u) + dot_nn(lower, gr_l)
-                value = g[h, 0, rows, cols].astype(F32) * zr + g[h, 1, rows, cols].astype(F32) * zi
+                cols = slice(t * step, (t + 1) * step)
+                zr = dot_nn(upper, g[h, 0, lo:, cols]) - dot_nn(lower, g[h, 1, :hi, cols])
+                zi = dot_nn(upper, g[h, 1, lo:, cols]) + dot_nn(lower, g[h, 0, :hi, cols])
+                value = g[h, 0, lo:hi, cols].astype(F32) * zr
+                value += g[h, 1, lo:hi, cols].astype(F32) * zi
                 value = jnp.sum(value, axis=0, keepdims=True)
-                if w > 0:
+                if lo > 0:
                     value = value + sens[h, :, cols]
                 sens[h, :, cols] = value
 
-    stages = (produce, pass_on, collect, finish, share, forward, consume)
-    for slot in range(WAVES + len(stages) - 1):
-        for s, stage in enumerate(stages):
-            if 0 <= slot - s < WAVES:
-                stage(slot - s)
+    def step_of(fa, fb):
+        def run(group):
+            for c in range(*group):
+                (fa if KINDS[c] == "A" else fb)(c)
+
+        return run
+
+    stages = (
+        produce,
+        step_of(pass_on, b_sum),
+        step_of(collect, b_pass_on),
+        step_of(finish, b_finish),
+        step_of(share, b_forward),
+        step_of(forward, b_last),
+        consume,
+    )
+    for slot in range(len(GROUPS) + len(stages) - 1):
+        for n, stage in enumerate(stages):
+            if 0 <= slot - n < len(GROUPS):
+                stage(GROUPS[slot - n])
 
     f_copies = []
     me = q * 2 + core
@@ -306,45 +451,56 @@
     return pl.pallas_call(
         functools.partial(kernel, nfreq),
         out_shape=jax.ShapeDtypeStruct((1, cells), F32),
-        in_specs=[
-            pl.BlockSpec(memory_space=pl.ANY),
-            pl.BlockSpec(memory_space=pltpu.VMEM),
-            pl.BlockSpec(memory_space=pltpu.SMEM),
-            pl.BlockSpec(memory_space=pltpu.VMEM),
-            pl.BlockSpec(memory_space=pltpu.SMEM),
-        ],
+        in_specs=[pl.BlockSpec(memory_space=pltpu.HBM)] * 5,
         out_specs=pl.BlockSpec(memory_space=pltpu.VMEM),
         scratch_shapes=[
+            pltpu.SMEM(basis.shape, F32),
+            pltpu.VMEM(amplitude.shape, F32),
+            pltpu.SMEM(block_mask.shape, jnp.int32),
             pltpu.VMEM((2, 2, NS, cells), BF16),
             pltpu.VMEM((nfreq, 2, 1, cells), F32),
-            pltpu.VMEM((2, 2, ROWS, cells), BF16),
-            pltpu.VMEM((WAVES, 8, UNIT, NS), BF16),
-            pltpu.VMEM((WAVES, 2, UNIT, NS), BF16),
-            pltpu.VMEM((WAVES, 2, UNIT, NS), BF16),
-            pltpu.VMEM((WAVES, 2, UNIT, NS), BF16),
-            pltpu.VMEM((WAVES, 2, UNIT, NS), BF16),
-            pltpu.VMEM((WAVES, UNIT, NS), BF16),
-            pltpu.VMEM((WAVES, UNIT, NS), BF16),
-            pltpu.VMEM((WAVES, UNIT, NS), F32),
-            pltpu.VMEM((WAVES, 8, UNIT, NS), BF16),
-            pltpu.VMEM((WAVES, UNIT, NS), F32),
+            pltpu.VMEM((2, 2, 2 * ROWS, cells), BF16),
+            pltpu.VMEM((CHUNKS, 8, UNIT, NS), BF16),
+            pltpu.VMEM((CHUNKS, 8, UNIT, NS), BF16),
+            pltpu.VMEM((CHUNKS, UNIT, NS), F32),
+            pltpu.VMEM((CHUNKS, UNIT, NS), F32),
+            pltpu.VMEM((CHUNKS, 2, UNIT, NS), BF16),
+            pltpu.VMEM((CHUNKS, 2, UNIT, NS), BF16),
+            pltpu.VMEM((CHUNKS, 2, UNIT, NS), BF16),
+            pltpu.VMEM((CHUNKS, 2, UNIT, NS), BF16),
+            pltpu.VMEM((CHUNKS, UNIT, NS), BF16),
+            pltpu.VMEM((CHUNKS, UNIT, NS), BF16),
+            pltpu.VMEM((CHUNKS, 4, UNIT, NS), BF16),
+            pltpu.VMEM((CHUNKS, 3, UNIT, NS), BF16),
+            pltpu.VMEM((CHUNKS, 2, UNIT, HALF), BF16),
+            pltpu.VMEM((CHUNKS, 2, UNIT, HALF), BF16),
+            pltpu.VMEM((CHUNKS, 2, UNIT, HALF), BF16),
+            pltpu.VMEM((CHUNKS, 2, UNIT, HALF), F32),
+            pltpu.VMEM((CHUNKS, 2, UNIT, HALF), BF16),
             pltpu.VMEM((2, 1, cells), F32),
             pltpu.VMEM((n, 1, cells), F32),
             pltpu.VMEM((2 * nfreq, 1, cells), F32),
+            dma((4,)),
             dma((2,)),
             dma((2,)),
             dma((2,)),
             dma((n,)),
             dma((n,)),
-            dma((WAVES, 4, 2)),
-            dma((WAVES, 4, 2)),
-            dma((WAVES, 7)),
-            dma((WAVES, 8)),
+            dma((CHUNKS, 4, 2)),
+            dma((CHUNKS, 4, 2)),
+            dma((CHUNKS, 7)),
+            dma((CHUNKS, 8)),
+            dma((CHUNKS, 4)),
+            dma((CHUNKS, 4)),
+            dma((CHUNKS, 3, 2)),
+            dma((CHUNKS, 3, 2)),
+            dma((CHUNKS, 8)),
+            dma((CHUNKS, 8)),
             dma((n,)),
             dma((n,)),
         ],
         compiler_params=pltpu.CompilerParams(
-            collective_id=0, has_side_effects=True, vmem_limit_bytes=48 * 1024 * 1024
+            collective_id=0, has_side_effects=True, vmem_limit_bytes=67043328
         ),
         name="hessian_vector",
     )(green, coeffs, basis, amplitude, block_mask)

time: 68.8 us -> 63.4 us (0.922)
  local copies, waits for them, and re-layouts: 5.52 us -> 1.26 us
  Pallas kernels: 63 us -> 62 us
    unnamed x11 -> x1, local copies, waits for them, and re-layouts: 5.52 us -> 1.26 us
    pallas_call x1, Pallas kernels: 63 us -> 62 us  [on_device(): pl.pallas_call(functools.partial(kernel, nfreq), out_shape=jax.ShapeDtype...]
where the time goes in v2:
time: 63.4 us; the launch traced here: 63.3 us
  Pallas kernels  62 us (98%)
  local copies, waits for them, and re-layouts  1.26 us (2%)
    pallas_call x1, Pallas kernels, on_device(): pl.pallas_call(functools.partial(kernel, nfreq), out_shape=jax.ShapeDtype...  62 us

profile of v2, /device:TPU:1, one launch (start us, length us, event | category | flops | bytes accessed | tf_op | source)
XLA Modules:
  0.0 63.3 jit_solution(14427943241213340202)
XLA Ops:
  0.0 62.0 %hessian_vector.1 = f32[1,512]{1,0:T(1,128)} custom-call(bf16[2,2,1024,512]{3,2,1,0:T(8,128)(2,1)} %green.1, f32[1,512]{1,0:T(1,128)} %coeffs.1, f32[2,8]{1,0:T(2,128)} %basis_in.1, f32[2,1024]{1,0:T(2,128)} %amp_in.1, s32[16,16]{1,0:T(8,128)} %mask_in.1), custom_call_target="tpu_custom_call" | custom-call | tf_op jit(solution)/shard_map/hessian_vector/pallas_call | solution.py:451
  62.0 1.3 %copy.7 = f32[1,512]{1,0:T(1,128)} copy(f32[1,512]{1,0:T(1,128)} %hessian_vector.1) | data formatting | bytes 4096

commit v3 on v2

--- a/solution.py
+++ b/solution.py
@@ -13,9 +13,21 @@
 ROWS = 128
 UNIT = ROWS // 8
 HALF = NS // 2
-KINDS = "ABABABAB"
+KINDS = "BAABABAB"
 GROUPS = ((0, 2), (2, 4), (4, 6), (6, 8))
 CHUNKS = len(KINDS)
+ORDER = (
+    ("P", 0), ("P", 1), ("P", 2), ("B0", 0), ("A1u", 1), ("A1d", 1), ("P", 3), ("B3", 0),
+    ("B1", 0), ("B2", 0), ("A1u", 2), ("A1d", 2), ("B0", 3), ("B1", 3), ("A1u", 4), ("A1d", 4),
+    ("B2", 3), ("B4u", 0), ("B4d", 0), ("B3", 3), ("A2", 1), ("B0", 5), ("A1u", 6), ("A1d", 6),
+    ("B1", 5), ("B2", 5), ("B3", 5), ("A2", 2), ("B4u", 3), ("B4d", 3), ("B0", 7), ("B1", 7),
+    ("A2", 4), ("B5", 0), ("B2", 7), ("B4u", 5), ("B4d", 5), ("B3", 7), ("A2", 6), ("A3", 1),
+    ("B5", 3), ("B4u", 7), ("B4d", 7), ("A3", 2), ("A3", 4), ("B6u", 0), ("B6d", 0), ("B5", 5),
+    ("A3", 6), ("A4", 1), ("B6u", 3), ("B6d", 3), ("B5", 7), ("A4", 2), ("A4", 4), ("B7", 0),
+    ("B6u", 5), ("B6d", 5), ("A5u", 1), ("A5d", 1), ("A4", 6), ("B7", 3), ("B6u", 7),
+    ("B6d", 7), ("A5u", 2), ("A5d", 2), ("A5u", 4), ("A5d", 4), ("B7", 5), ("C", 0), ("A5u", 6),
+    ("A5d", 6), ("B7", 7), ("C", 1), ("C", 2), ("C", 3),
+)
 BLOCKS = 16
 WIDTH = NS // BLOCKS
 
@@ -94,7 +106,8 @@
     up, down = at(x, yp, core), at(x, ym, core)
     across, twin = at(1 - x, y, core), at(x, y, 1 - core)
 
-    peers = [(d, h) for d in range(nfreq) for h in range(2) if (d, h) != (0, 0)]
+    far_first = sorted(range(nfreq), key=lambda d: (d % 4 != 2, d % 2 == 0, d == 0))
+    peers = [(d, h) for d in far_first for h in (1, 0) if (d, h) != (0, 0)]
 
     def peer(d, h):
         to_core = core if h == 0 else 1 - core
@@ -268,28 +281,36 @@
         for r in range(4):
             start(b_cross(w, r))
 
-    def b_sum(w):
-        def total(r):
-            b_cross(w, r).wait_recv()
-            return part[w, targets[r] * 2 + x].astype(F32) + bx[w, r].astype(F32)
-
-        bsum[w, 0] = total(0).astype(BF16)
+    def b_total(w, r):
+        b_cross(w, r).wait_recv()
+        return part[w, targets[r] * 2 + x].astype(F32) + bx[w, r].astype(F32)
+
+    def b_sum_far(w):
+        bsum[w, 0] = b_total(w, 0).astype(BF16)
         start(b_up(w, 0, left(bsum.at[w, 0]), b1.at[w, 0]))
         start(b_down(w, 0, right(bsum.at[w, 0]), b1.at[w, 1]))
-        value = total(1)
+
+    def b_sum_up(w):
+        value = b_total(w, 1)
         bhold[w, 0] = value[:, :HALF]
         bsum[w, 1, :, HALF:] = value[:, HALF:].astype(BF16)
         start(b_up(w, 1, right(bsum.at[w, 1]), b2.at[w, 0]))
-        value = total(2)
+
+    def b_sum_down(w):
+        value = b_total(w, 2)
         bhold[w, 1] = value[:, HALF:]
         bsum[w, 2, :, :HALF] = value[:, :HALF].astype(BF16)
         start(b_down(w, 1, left(bsum.at[w, 2]), b2.at[w, 1]))
-        keep[w] = total(3)
-
-    def b_pass_on(w):
+
+    def b_sum_own(w):
+        keep[w] = b_total(w, 3)
+
+    def b_relay_up(w):
         b_up(w, 0, left(bsum.at[w, 0]), b1.at[w, 0]).wait_recv()
         brelay[w, 0] = (bhold[w, 0] + b1[w, 0].astype(F32)).astype(BF16)
         start(b_up(w, 2, brelay.at[w, 0], b3.at[w, 0]))
+
+    def b_relay_down(w):
         b_down(w, 0, right(bsum.at[w, 0]), b1.at[w, 1]).wait_recv()
         brelay[w, 1] = (bhold[w, 1] + b1[w, 1].astype(F32)).astype(BF16)
         start(b_down(w, 2, brelay.at[w, 1], b3.at[w, 1]))
@@ -308,10 +329,12 @@
         start(b_share(w, 1, b_unit(w, y), down))
         start(b_share(w, 4, b_unit(w, y), across))
 
-    def b_forward(w):
+    def b_forward_up(w):
         b_share(w, 0, b_unit(w, ym), up).wait_recv()
         start(b_share(w, 2, left(b_unit(w, ym)), up))
         start(b_share(w, 5, b_unit(w, ym), across))
+
+    def b_forward_down(w):
         b_share(w, 1, b_unit(w, yp), down).wait_recv()
         start(b_share(w, 3, right(b_unit(w, yp)), down))
         start(b_share(w, 6, b_unit(w, yp), across))
@@ -321,10 +344,12 @@
         b_share(w, 3, right(b_unit(w, y2)), down).wait_recv()
         start(b_share(w, 7, b_unit(w, y2), across))
 
-    def pass_on(w):
+    def a_relay_up(w):
         rs_up(w, 0, part.at[w, y2 * 2], m1.at[w, 0]).wait_recv()
         relay[w, 0] = (part[w, yp * 2].astype(F32) + m1[w, 0].astype(F32)).astype(BF16)
         start(rs_up(w, 2, relay.at[w, 0], m3.at[w, 0]))
+
+    def a_relay_down(w):
         rs_down(w, 0, part.at[w, y2 * 2 + 1], m1.at[w, 1]).wait_recv()
         relay[w, 1] = (part[w, ym * 2 + 1].astype(F32) + m1[w, 1].astype(F32)).astype(BF16)
         start(rs_down(w, 2, relay.at[w, 1], m3.at[w, 1]))
@@ -358,9 +383,11 @@
         start(ag(w, 3, unit, up))
         start(ag(w, 4, unit, down))
 
-    def forward(w):
+    def forward_up(w):
         ag(w, 1, ym * 2, up).wait_recv()
         start(ag(w, 5, ym * 2, up))
+
+    def forward_down(w):
         ag(w, 1, yp * 2 + 1, down).wait_recv()
         start(ag(w, 6, yp * 2 + 1, down))
 
@@ -403,26 +430,29 @@
                     value = value + sens[h, :, cols]
                 sens[h, :, cols] = value
 
-    def step_of(fa, fb):
-        def run(group):
-            for c in range(*group):
-                (fa if KINDS[c] == "A" else fb)(c)
-
-        return run
-
-    stages = (
-        produce,
-        step_of(pass_on, b_sum),
-        step_of(collect, b_pass_on),
-        step_of(finish, b_finish),
-        step_of(share, b_forward),
-        step_of(forward, b_last),
-        consume,
-    )
-    for slot in range(len(GROUPS) + len(stages) - 1):
-        for n, stage in enumerate(stages):
-            if 0 <= slot - n < len(GROUPS):
-                stage(GROUPS[slot - n])
+    ops = {
+        "P": lambda n: produce(GROUPS[n]),
+        "C": lambda n: consume(GROUPS[n]),
+        "A1u": a_relay_up,
+        "A1d": a_relay_down,
+        "A2": collect,
+        "A3": finish,
+        "A4": share,
+        "A5u": forward_up,
+        "A5d": forward_down,
+        "B0": b_sum_far,
+        "B1": b_sum_up,
+        "B2": b_sum_down,
+        "B3": b_sum_own,
+        "B4u": b_relay_up,
+        "B4d": b_relay_down,
+        "B5": b_finish,
+        "B6u": b_forward_up,
+        "B6d": b_forward_down,
+        "B7": b_last,
+    }
+    for name, n in ORDER:
+        ops[name](n)
 
     f_copies = []
     me = q * 2 + core

time: 63.4 us -> 61.6 us (0.972)
  Pallas kernels: 62 us -> 60.2 us
    pallas_call x1, Pallas kernels: 62 us -> 60.2 us  [on_device(): pl.pallas_call(functools.partial(kernel, nfreq), out_shape=jax.ShapeDtype...]
where the time goes in v3:
time: 61.6 us; the launch traced here: 61.5 us
  Pallas kernels  60.2 us (98%)
  local copies, waits for them, and re-layouts  1.26 us (2%)
    pallas_call x1, Pallas kernels, on_device(): pl.pallas_call(functools.partial(kernel, nfreq), out_shape=jax.ShapeDtype...  60.2 us
    unnamed x1, local copies, waits for them, and re-layouts  1.26 us

profile of v3, /device:TPU:1, one launch (start us, length us, event | category | flops | bytes accessed | tf_op | source)
XLA Modules:
  0.0 61.5 jit_solution(4686037004728736195)
XLA Ops:
  0.0 60.2 %hessian_vector.1 = f32[1,512]{1,0:T(1,128)} custom-call(bf16[2,2,1024,512]{3,2,1,0:T(8,128)(2,1)} %green.1, f32[1,512]{1,0:T(1,128)} %coeffs.1, f32[2,8]{1,0:T(2,128)} %basis_in.1, f32[2,1024]{1,0:T(2,128)} %amp_in.1, s32[16,16]{1,0:T(8,128)} %mask_in.1), custom_call_target="tpu_custom_call" | custom-call | tf_op jit(solution)/shard_map/hessian_vector/pallas_call | solution.py:481
  60.2 1.3 %copy.7 = f32[1,512]{1,0:T(1,128)} copy(f32[1,512]{1,0:T(1,128)} %hessian_vector.1) | data formatting | bytes 4096

commit v4 on v3

--- a/solution.py
+++ b/solution.py
@@ -141,7 +141,23 @@
     for device in met:
         pl.semaphore_signal(barrier, inc=1, device_id=device, device_id_type=MESH)
 
-    for copy in small:
+    small[3].wait()
+    pl.semaphore_wait(barrier, len(met))
+
+    c_copies = []
+    for n, (d, h) in enumerate(peers):
+        c_copies.append(
+            remote(cbuf.at[q, 0], cbuf.at[q, h], c_send.at[n], c_recv.at[n], peer(d, h))
+        )
+        c_copies[-1].start()
+    swap = [
+        remote(green.at[p, 1 - core], g.at[1, p], swap_send.at[p], swap_recv.at[p], twin)
+        for p in range(2)
+    ]
+    for copy in swap:
+        copy.start()
+
+    for copy in small[:3]:
         copy.wait()
 
     lane = lax.broadcasted_iota(jnp.int32, (1, NS), 1)
@@ -159,21 +175,6 @@
         same = row == col
         amp_col = jnp.sum(jnp.where(same, amp_row, 0.0), axis=1, keepdims=True)
         weight[w] = jnp.where(same, 0.5, 1.0) * (amp_col * (amp_row * pair))
-
-    pl.semaphore_wait(barrier, len(met))
-
-    c_copies = []
-    for n, (d, h) in enumerate(peers):
-        c_copies.append(
-            remote(coeffs, cbuf.at[q, h], c_send.at[n], c_recv.at[n], peer(d, h))
-        )
-        c_copies[-1].start()
-    swap = [
-        remote(green.at[p, 1 - core], g.at[1, p], swap_send.at[p], swap_recv.at[p], twin)
-        for p in range(2)
-    ]
-    for copy in swap:
-        copy.start()
 
     for copy in c_copies:
         copy.wait_recv()

time: 61.6 us -> 61.4 us (level)
  no operation moved by 1% of the time
where the time goes in v4:
time: 61.4 us; the launch traced here: 61.2 us
  Pallas kernels  60 us (98%)
  local copies, waits for them, and re-layouts  1.26 us (2%)
    pallas_call x1, Pallas kernels, on_device(): pl.pallas_call(functools.partial(kernel, nfreq), out_shape=jax.ShapeDtype...  60 us
    unnamed x1, local copies, waits for them, and re-layouts  1.26 us

profile of v4, /device:TPU:1, one launch (start us, length us, event | category | flops | bytes accessed | tf_op | source)
XLA Modules:
  0.0 61.2 jit_solution(2078257213320958353)
XLA Ops:
  0.0 60.0 %hessian_vector.1 = f32[1,512]{1,0:T(1,128)} custom-call(bf16[2,2,1024,512]{3,2,1,0:T(8,128)(2,1)} %green.1, f32[1,512]{1,0:T(1,128)} %coeffs.1, f32[2,8]{1,0:T(2,128)} %basis_in.1, f32[2,1024]{1,0:T(2,128)} %amp_in.1, s32[16,16]{1,0:T(8,128)} %mask_in.1), custom_call_target="tpu_custom_call" | custom-call | tf_op jit(solution)/shard_map/hessian_vector/pallas_call | solution.py:482
  60.0 1.3 %copy.7 = f32[1,512]{1,0:T(1,128)} copy(f32[1,512]{1,0:T(1,128)} %hessian_vector.1) | data formatting | bytes 4096

commit v5 on v4

--- a/solution.py
+++ b/solution.py
@@ -187,8 +187,6 @@
 
     for copy in own:
         copy.wait()
-    for copy in swap:
-        copy.wait_recv()
 
     sent = []
 
@@ -211,6 +209,9 @@
         lo, hi = c0 * ROWS, c1 * ROWS
         count = hi - lo
         for h in range(2):
+            if c0 == 0 and h == 1:
+                for copy in swap:
+                    copy.wait_recv()
             for p in range(2):
                 field = g[h, p, lo:hi, :].astype(F32)
                 sc[h, p, :count, :] = (field * source[h]).astype(BF16)

time: 61.4 us -> 61.5 us (level)
  no operation moved by 1% of the time
where the time goes in v5:
time: 61.5 us; the launch traced here: 61.3 us
  Pallas kernels  60 us (98%)
  local copies, waits for them, and re-layouts  1.26 us (2%)
    pallas_call x1, Pallas kernels, on_device(): pl.pallas_call(functools.partial(kernel, nfreq), out_shape=jax.ShapeDtype...  60 us
    unnamed x1, local copies, waits for them, and re-layouts  1.26 us

profile of v5, /device:TPU:1, one launch (start us, length us, event | category | flops | bytes accessed | tf_op | source)
XLA Modules:
  0.0 61.3 jit_solution(1746290479914952308)
XLA Ops:
  0.0 60.0 %hessian_vector.1 = f32[1,512]{1,0:T(1,128)} custom-call(bf16[2,2,1024,512]{3,2,1,0:T(8,128)(2,1)} %green.1, f32[1,512]{1,0:T(1,128)} %coeffs.1, f32[2,8]{1,0:T(2,128)} %basis_in.1, f32[2,1024]{1,0:T(2,128)} %amp_in.1, s32[16,16]{1,0:T(8,128)} %mask_in.1), custom_call_target="tpu_custom_call" | custom-call | tf_op jit(solution)/shard_map/hessian_vector/pallas_call | solution.py:483
  60.1 1.3 %copy.7 = f32[1,512]{1,0:T(1,128)} copy(f32[1,512]{1,0:T(1,128)} %hessian_vector.1) | data formatting | bytes 4096
